TPU v7x, 32 devices: a whole 2x2x4 slice. The times are simulated.
32 devices in a mesh: dp: 4 (over y, core), owner: 8 (over z, x).
Axes of the slice: x: 2, y: 2, z: 4, core: 2. Of those that a mesh axis runs over, the one named last changes fastest.
Arguments:
- embeddings: bfloat16 [131072, 1024], P(('dp', 'owner')), may hold values from -40 to 40, as said below
- cluster_ids: int32 [131072, 1], P(('dp', 'owner')), may hold values from 0 to 63; in each aligned block of 4096 rows (0 to 4095, 4096 to 8191, ...) at most 128 rows name the same one
- noise: bfloat16 [131072, 256], P(('dp', 'owner')), may hold values from -3 to 3
- start_basis: float32 [1024, 256], replicated, may hold values from -0.1875 to 0.1875
Outputs:
- routed: bfloat16 [4, 64, 8, 128, 256], P('dp', 'owner')
Inputs may be any that keep to these rules, and one draw needn't show every extreme that they name: `embeddings`: entries are of order one around a column mean. `cluster_ids`: no cluster holds more than 128 rows of one device, and some cluster holds exactly 128 rows of some device.
All inputs are finite; a program needn't handle non-finite values.
Results may differ from a plain program's by a relative error of at most 0.0046.
Values may be sent and summed in bfloat16 or wider, within the bound.
No kernel may reach another device: no remote copies, remote signals or barrier semaphores. Data moves between devices by JAX's collectives and lax.ppermute only.
A program may use at most 128 MiB of HBM per device.

v0:
```python
import math
import jax
import jax.numpy as jnp
from jax import lax
from jax.sharding import PartitionSpec as P

CL_DEV = 8


def shards(embeddings, cluster_ids, noise, start_basis):
    highest = lax.Precision.HIGHEST
    rows_dev, feature_width = embeddings.shape
    rank_count = start_basis.shape[1]
    owners = lax.axis_size("owner")
    row_total = rows_dev * lax.axis_size("dp") * owners
    column_sum = jnp.sum(embeddings, axis=0, dtype=jnp.float32)
    second = lax.dot_general(
        embeddings, embeddings, (((0,), (0,)), ((), ())), preferred_element_type=jnp.float32
    )
    second_all, column_all = lax.psum((second, column_sum), ("dp", "owner"))
    mean_vec = column_all / row_total
    covariance = second_all / row_total - jnp.outer(mean_vec, mean_vec)
    image_rows = jnp.dot(covariance, start_basis, precision=highest)
    gram_matrix = jnp.dot(image_rows.T, image_rows, precision=highest)
    lower_factor = jnp.linalg.cholesky(gram_matrix)
    basis_full = lax.linalg.triangular_solve(
        lower_factor, image_rows, left_side=False, lower=True, transpose_a=True
    )
    curved = jnp.dot(covariance, basis_full, precision=highest)
    eigen_vals = jnp.sum(basis_full * curved, axis=0)
    signed = math.sqrt(feature_width) * jnp.sum(basis_full, axis=0)
    flip_sign = signed / jnp.maximum(jnp.abs(signed), 1.0)
    whiten = (basis_full * (flip_sign / jnp.sqrt(eigen_vals + 1e-06))).astype(jnp.bfloat16)
    offset = jnp.dot(mean_vec, whiten.astype(jnp.float32), precision=highest)
    clusters = CL_DEV * owners
    capacity = 2 * rows_dev // clusters
    ids_here = cluster_ids[:, 0]
    onehot = (cluster_ids == jnp.arange(clusters, dtype=jnp.int32)[None, :]).astype(jnp.int32)
    before = jnp.cumsum(onehot, axis=0) - onehot
    slot_index = jnp.sum(before * onehot, axis=1)
    destination = ids_here * capacity + slot_index
    projected = (
        jnp.dot(embeddings, whiten, preferred_element_type=jnp.float32)
        - offset
        + noise.astype(jnp.float32)
    ).astype(jnp.bfloat16)
    packed = (
        jnp.zeros((clusters * capacity, rank_count), jnp.bfloat16).at[destination].set(projected)
    )
    packed = packed.reshape(clusters, 1, capacity, rank_count)
    arrived = lax.all_to_all(packed, "owner", split_axis=0, concat_axis=1, tiled=True)
    return arrived[None]


def solution(mesh):
    return jax.shard_map(
        shards,
        mesh=mesh,
        in_specs=(
            P(("dp", "owner"), None),
            P(("dp", "owner"), None),
            P(("dp", "owner"), None),
            P(),
        ),
        out_specs=P("dp", "owner", None, None, None),
        check_vma=False,
    )
```

profile of v0, /device:TPU:0, one launch (start us, length us, event | category | flops | bytes accessed | tf_op | source)
XLA Modules:
  0.0 376.8 jit_solution(5720101799312781308)
XLA Ops:
  6.5 0.0 copy-start
  6.5 0.0 all-reduce.3.cloned.1.call-start
  6.5 15.1 %fusion.32 = f32[1024,1024]{1,0:T(8,128)} fusion(bf16[4096,1024]{1,0:T(8,128)(2,1)} %param.4), kind=kOutput, calls=%fused_computation.64 | convolution fusion | flops 8589934592 | bytes 12582912 | tf_op jit(solution)/shard_map/dot_general | solution.py:17
  21.6 0.0 all-reduce.3.cloned.1.call-update
  21.7 1.6 copy-done.2
  23.2 2.9 copy.20
  26.1 0.0 copy-done.4
  26.1 0.1 fusion.18
  26.3 18.4 %reduce-window.6 = s32[64,32,128]{2,1,0:T(8,128)S(1)} reduce-window(s32[64,32,128]{2,1,0:T(8,128)S(1)} %fusion.18, s32[]{:T(128)} %copy.38), window={size=1x1x128 pad=0_0x0_0x127_0}, to_apply=%region_0.0 | reduce-window | flops 33292288 | bytes 2097156 | tf_op jit(solution)/shard_map/reduce-window
  44.7 0.3 slice.61
  45.1 0.4 copy.25
  45.5 0.2 reduce-window.9
  45.7 4.7 %convert_reduce_fusion = f32[1024]{0:T(1024)S(1)} fusion(bf16[4096,1024]{1,0:T(8,128)(2,1)} %param.4), kind=kLoop, calls=%fused_computation.3 | loop fusion | flops 8387584 | bytes 8392704 | tf_op jit(solution)/shard_map/reduce_sum | solution.py:16
  50.4 42.3 %psum.15 = f32[1024]{0:T(1024)S(1)} all-reduce(f32[1024]{0:T(1024)S(1)} %convert_reduce_fusion), channel_id=1, replica_groups=mesh['dp'=4,'owner'=8] {'dp','owner'}, use_global_device_ids=true, to_apply=%region_5.6 | all-reduce | flops 1024 | bytes 8192 | tf_op jit(solution)/shard_map/psum | solution.py:20
  92.7 0.3 broadcast_add_fusion
  93.0 0.9 fusion.17
  94.0 73.1 %all-reduce.3.cloned.1.call-done = f32[1024,1024]{1,0:T(8,128)} async-done(((f32[1024,1024]{1,0:T(8,128)}), f32[1024,1024]{1,0:T(8,128)}) %all-reduce.3.cloned.1.call-update) | async-done | bytes 4194320 | tf_op jit(solution)/shard_map/psum | solution.py:20
  167.1 0.0 copy-done
  167.1 6.1 %fusion.4 = f32[1024,256]{1,0:T(8,128)S(1)} fusion(f32[1024,256]{1,0:T(8,128)S(1)} %copy-done, f32[1024,1024]{1,0:T(8,128)} %all-reduce.3.cloned.1.call-done, f32[1024]{0:T(1024)S(1)} %broadcast_multiply_fusion), kind=kOutput, calls=%fused_computation.10 | convolution fusion | flops 3224371200 | bytes 6295552 | tf_op jit(solution)/shard_map/dot_general | solution.py:23
  173.2 1.8 fusion.33
  175.0 0.1 copy.18
  175.2 11.7 %cholesky.50 = f32[128,128]{1,0:T(8,128)S(1)} custom-call(f32[128,128]{1,0:T(8,128)S(1)} %cholesky.118), custom_call_target="Cholesky" | custom-call | tf_op jit(solution)/shard_map/jit(cholesky)/cholesky | solution.py:25
  187.0 9.8 %custom-call.14 = f32[1,128,128]{1,2,0:T(8,128)S(1)} custom-call(f32[1,128,128]{2,1,0:T(8,128)S(1)} %get-tuple-element.26), custom_call_target="InvertDiagBlocksLowerTriangular" | custom-call | tf_op jit(solution)/shard_map/jit(cholesky)/cholesky | solution.py:25
  196.8 0.2 constant_dynamic-update-slice_fusion.1
  197.0 0.3 convolution_subtract_fusion.2
  197.3 11.7 %cholesky.105 = f32[128,128]{1,0:T(8,128)S(1)} custom-call(f32[128,128]{1,0:T(8,128)S(1)} %convolution_subtract_fusion.2), custom_call_target="Cholesky" | custom-call | tf_op jit(solution)/shard_map/jit(cholesky)/cholesky | solution.py:25
  209.0 0.7 compare_reduce_fusion
  211.2 0.1 triangular_solve.58
  211.3 4.0 %while.1 = (s32[]{:T(128)}, f32[256,256]{1,0:T(8,128)S(1)}, s32[2,2]{1,0:T(2,128)S(1)}, f32[2,128,128]{2,1,0:T(8,128)S(1)}, s32[]{:T(128)}) while((s32[]{:T(128)}, f32[256,256]{1,0:T(8,128)S(1)}, s32[2,2]{1,0:T(2,128)S(1)}, f32[2,128,128]{2,1,0:T(8,128)S(1)}, s32[]{:T(128)}) %tuple.23), condition=%wide.while_cond, body=%wide.while_body.sunk | while | flops 2 | bytes 131181 | solution.py:26
  211.3 0.6 fusion.49
  211.9 1.4 bitcast_dynamic-update-slice_fusion.2
  213.3 0.6 fusion.49
  213.9 1.4 bitcast_dynamic-update-slice_fusion.2
  215.3 19.7 %custom-call.15 = f32[2,128,128]{1,2,0:T(8,128)S(1)} custom-call(f32[2,128,128]{2,1,0:T(8,128)S(1)} %get-tuple-element.12), custom_call_target="InvertDiagBlocksLowerTriangular" | custom-call | tf_op jit(solution)/shard_map/triangular_solve | solution.py:26
  234.9 0.0 copy-start.1
  235.0 0.6 fusion.20
  235.6 1.0 convolution_subtract_fusion.1
  236.6 0.6 fusion.23
  237.2 0.2 fusion.19
  237.4 0.0 copy-done.1
  237.4 4.5 %fusion.14 = f32[256]{0:T(256)S(1)} fusion(f32[1024,1024]{1,0:T(8,128)S(1)} %copy-done.1, f32[1024]{0:T(1024)S(1)} %broadcast_multiply_fusion, f32[1024,128]{0,1:T(8,128)S(1)} %fusion.23, f32[1024,128]{0,1:T(8,128)S(1)} %fusion.20), kind=kOutput, calls=%fused_computation.20 | convolution fusion | flops 3225157376 | bytes 5248000 | tf_op jit(solution)/shard_map/dot_general | solution.py:29
  241.9 0.1 multiply_convert_fusion
  242.0 0.5 fusion.34
  242.5 5.8 %fusion.2 = bf16[4096,256]{0,1:T(8,128)(2,1)S(1)} fusion(bf16[1024,256]{0,1:T(8,128)(2,1)S(1)} %multiply_convert_fusion, bf16[4096,1024]{1,0:T(8,128)(2,1)} %param.4, bf16[4096,256]{0,1:T(8,128)(2,1)S(1)} %copy-done.3, f32[256]{0:T(256)S(1)} %bitcast.90), kind=kOutput, calls=%fused_computation.7 | convolution fusion | flops 2151677952 | bytes 13108224 | tf_op jit(solution)/shard_map/dot_general | solution.py:43
  248.3 2.7 copy.21
  251.0 20.9 %scatter_custom_fusion = bf16[8192,256]{1,0:T(8,128)(2,1)} fusion(s32[4096]{0:T(1024)S(1)} %bitcast.89, bf16[4096,256]{1,0:T(8,128)(2,1)} %copy.21, bf16[]{:T(256)} %constant.88.clone.1), kind=kCustom, calls=%fused_computation.17 | custom fusion | bytes 4194816 | tf_op jit(solution)/shard_map/scatter | solution.py:48
  272.0 95.5 %all_to_all.15 = bf16[64,1,128,256]{3,2,1,0:T(8,128)(2,1)S(1)} all-to-all(bf16[64,1,128,256]{3,2,1,0:T(8,128)(2,1)} %bitcast.80), channel_id=1, replica_groups=mesh['dp'=4,'owner'=8] {'owner'}, dimensions={0} | all-to-all | bytes 8388608 | tf_op jit(solution)/shard_map/all_to_all | solution.py:51
  367.5 2.3 copy.23
  (17 shorter events, 0.2 us)
Async XLA Ops:
  6.5 160.6 %copy-start = (f32[1024,256]{1,0:T(8,128)S(1)}, f32[1024,256]{1,0:T(8,128)}, u32[]{:S(2)}) copy-start(f32[1024,256]{1,0:T(8,128)} %param.7) | copy-start | bytes 3145732
  6.5 160.6 %all-reduce.3.cloned.1.call-start = ((), (), s32[]{:S(2)}) async-start(), calls=%async_computation.1 | async-start | bytes 8388608 | tf_op jit(solution)/shard_map/psum | solution.py:20
  21.6 1.6 copy-start.2
  21.6 4.5 %copy-start.4 = (s32[4096,1]{0,1:T(1,128)S(1)}, s32[4096,1]{0,1:T(1,128)}, u32[]{:S(2)}) copy-start(s32[4096,1]{0,1:T(1,128)} %param.5) | copy-start | bytes 49156
  234.9 2.4 copy-start.1
  237.4 5.1 %copy-start.3 = (bf16[4096,256]{0,1:T(8,128)(2,1)S(1)}, bf16[4096,256]{0,1:T(8,128)(2,1)}, u32[]{:S(2)}) copy-start(bf16[4096,256]{0,1:T(8,128)(2,1)} %copy.20) | copy-start | bytes 6291460
Sparse Core Ops, SparseCore 0:
  21.8 145.2 all-reduce.2
where the time goes:
time: 385 us; the launch traced here: 377 us
  blocking collectives  138 us (36%)
  other arithmetic  78.7 us (20%)
  waiting for transfers between devices  73.2 us (19%)
  matrix products  36.5 us (9%)
  local copies, waits for them, and re-layouts  35.3 us (9%)
  between operations  15.3 us (4%)
    all_to_all x1, blocking collectives, shards(): lax.all_to_all(packed, 'owner', split_axis=0, concat_axis=1, tiled=True)  95.5 us
    psum x1, waiting for transfers between devices, shards(): second_all, column_all = lax.psum((second, column_sum), ('dp', 'owner'))  73.1 us
    psum x1, blocking collectives, shards(): second_all, column_all = lax.psum((second, column_sum), ('dp', 'owner'))  42.3 us
    another operation x6, other arithmetic, shards(): lower_factor = jnp.linalg.cholesky(gram_matrix)  34 us
    scatter x1, local copies, waits for them, and re-layouts, shards(): jnp.zeros((clusters * capacity, rank_count), jnp.bfloat16).at[destination]  20.9 us
    another operation x3, other arithmetic, shards(): lax.linalg.triangular_solve(lower_factor, image_rows, left_side=False, lo...  19.7 us
    another operation x3, other arithmetic  19 us
    dot_general x1, matrix products, shards(): lax.dot_general(embeddings, embeddings, (((0,), (0,)), ((), ())), preferr...  15.1 us
  transfers between devices with their start and end apart: 1, of which 1 were waited for; matrix products, arithmetic and copies ran while one was open for 8% of the time, Pallas kernels for 0%

commit v1 on v0

--- a/solution.py
+++ b/solution.py
@@ -17,7 +17,7 @@
     second = lax.dot_general(
         embeddings, embeddings, (((0,), (0,)), ((), ())), preferred_element_type=jnp.float32
     )
-    second_all, column_all = lax.psum((second, column_sum), ("dp", "owner"))
+    second_all, column_all = lax.psum(lax.psum((second, column_sum), "dp"), "owner")
     mean_vec = column_all / row_total
     covariance = second_all / row_total - jnp.outer(mean_vec, mean_vec)
     image_rows = jnp.dot(covariance, start_basis, precision=highest)

time: 385 us -> 489 us (1.27)
  waiting for transfers between devices: 73.2 us -> 192 us
  blocking collectives: 138 us -> 126 us
    psum x1 -> x2, waiting for transfers between devices: 73.1 us -> 192 us  [the longest x1 103 us: shards(): lax.psum(lax.psum((second, column_sum), 'dp'), 'owner')]
    psum x1 -> x2, blocking collectives: 42.3 us -> 28.8 us  [the longest x1 22.6 us: shards(): lax.psum(lax.psum((second, column_sum), 'dp'), 'owner')]
  transfers between devices with their start and end apart: 1 -> 2, of which waited for: 1 -> 2; matrix products, arithmetic and copies ran while one was open for 8% -> 6% of each run, Pallas kernels for 0% -> 0%
where the time goes in v1:
time: 489 us; the launch traced here: 482 us
  waiting for transfers between devices  192 us (39%)
  blocking collectives  126 us (26%)
  other arithmetic  78.7 us (16%)
  matrix products  36.5 us (7%)
  local copies, waits for them, and re-layouts  33.6 us (7%)
  between operations  15.2 us (3%)
    psum x1, waiting for transfers between devices, shards(): lax.psum(lax.psum((second, column_sum), 'dp'), 'owner')  103 us
    all_to_all x1, blocking collectives, shards(): lax.all_to_all(packed, 'owner', split_axis=0, concat_axis=1, tiled=True)  96.9 us
    psum x1, waiting for transfers between devices, shards(): lax.psum((second, column_sum), 'dp')  88.3 us
    another operation x6, other arithmetic, shards(): lower_factor = jnp.linalg.cholesky(gram_matrix)  34 us
    psum x1, blocking collectives, shards(): lax.psum(lax.psum((second, column_sum), 'dp'), 'owner')  22.6 us
    scatter x1, local copies, waits for them, and re-layouts, shards(): jnp.zeros((clusters * capacity, rank_count), jnp.bfloat16).at[destination]  20.9 us
    another operation x3, other arithmetic, shards(): lax.linalg.triangular_solve(lower_factor, image_rows, left_side=False, lo...  19.7 us
    another operation x3, other arithmetic  19 us
  transfers between devices with their start and end apart: 2, of which 2 were waited for; matrix products, arithmetic and copies ran while one was open for 6% of the time, Pallas kernels for 0%

profile of v1, /device:TPU:0, one launch (start us, length us, event | category | flops | bytes accessed | tf_op | source)
XLA Modules:
  0.0 481.5 jit_solution(6318980991816182094)
XLA Ops:
  6.5 0.0 copy-start
  6.5 0.0 all-reduce.4.cloned.1.call-start
  6.5 15.1 %fusion.32 = f32[1024,1024]{1,0:T(8,128)} fusion(bf16[4096,1024]{1,0:T(8,128)(2,1)} %param.4), kind=kOutput, calls=%fused_computation.64 | convolution fusion | flops 8589934592 | bytes 12582912 | tf_op jit(solution)/shard_map/dot_general | solution.py:17
  21.6 0.0 all-reduce.4.cloned.1.call-update
  21.7 0.0 all-reduce.6.cloned.1.call-start
  21.7 88.3 %all-reduce.4.cloned.1.call-done = f32[1024,1024]{1,0:T(8,128)} async-done(((f32[1024,1024]{1,0:T(8,128)}), f32[1024,1024]{1,0:T(8,128)}) %all-reduce.4.cloned.1.call-update) | async-done | bytes 4194320 | tf_op jit(solution)/shard_map/psum | solution.py:20
  110.0 0.0 all-reduce.6.cloned.1.call-update
  110.1 2.9 copy.20
  112.9 0.1 fusion.18
  113.1 18.4 %reduce-window.6 = s32[64,32,128]{2,1,0:T(8,128)S(1)} reduce-window(s32[64,32,128]{2,1,0:T(8,128)S(1)} %fusion.18, s32[]{:T(128)} %copy.39), window={size=1x1x128 pad=0_0x0_0x127_0}, to_apply=%region_0.0 | reduce-window | flops 33292288 | bytes 2097156 | tf_op jit(solution)/shard_map/reduce-window
  131.5 0.3 slice.61
  131.9 0.4 copy.25
  132.3 0.2 reduce-window.9
  132.5 4.6 convert_reduce_fusion
  137.1 6.1 %psum.30 = f32[1024]{0:T(1024)S(1)} all-reduce(f32[1024]{0:T(1024)S(1)} %convert_reduce_fusion), channel_id=1, replica_groups=mesh['dp'=4,'owner'=8] {'dp'}, use_global_device_ids=true, to_apply=%region_6.7 | all-reduce | flops 1024 | bytes 8192 | tf_op jit(solution)/shard_map/psum | solution.py:20
  143.3 22.6 %psum.31 = f32[1024]{0:T(1024)S(1)} all-reduce(f32[1024]{0:T(1024)S(1)} %psum.30), channel_id=1, replica_groups=mesh['dp'=4,'owner'=8] {'owner'}, use_global_device_ids=true, to_apply=%region_7.8 | all-reduce | flops 1024 | bytes 8192 | tf_op jit(solution)/shard_map/psum | solution.py:20
  165.9 0.3 broadcast_add_fusion
  166.2 0.9 fusion.17
  167.2 103.4 %all-reduce.6.cloned.1.call-done = f32[1024,1024]{1,0:T(8,128)} async-done(((f32[1024,1024]{1,0:T(8,128)}), f32[1024,1024]{1,0:T(8,128)}) %all-reduce.6.cloned.1.call-update) | async-done | bytes 4194320 | tf_op jit(solution)/shard_map/psum | solution.py:20
  270.6 6.1 %fusion.4 = f32[1024,256]{1,0:T(8,128)S(1)} fusion(f32[1024,256]{1,0:T(8,128)S(1)} %copy-done, f32[1024,1024]{1,0:T(8,128)} %all-reduce.6.cloned.1.call-done, f32[1024]{0:T(1024)S(1)} %broadcast_multiply_fusion), kind=kOutput, calls=%fused_computation.10 | convolution fusion | flops 3224371200 | bytes 6295552 | tf_op jit(solution)/shard_map/dot_general | solution.py:23
  276.7 1.8 fusion.33
  278.5 0.1 copy.18
  278.7 11.7 %cholesky.50 = f32[128,128]{1,0:T(8,128)S(1)} custom-call(f32[128,128]{1,0:T(8,128)S(1)} %cholesky.118), custom_call_target="Cholesky" | custom-call | tf_op jit(solution)/shard_map/jit(cholesky)/cholesky | solution.py:25
  290.5 9.8 %custom-call.14 = f32[1,128,128]{1,2,0:T(8,128)S(1)} custom-call(f32[1,128,128]{2,1,0:T(8,128)S(1)} %get-tuple-element.26), custom_call_target="InvertDiagBlocksLowerTriangular" | custom-call | tf_op jit(solution)/shard_map/jit(cholesky)/cholesky | solution.py:25
  300.3 0.2 constant_dynamic-update-slice_fusion.1
  300.5 0.3 convolution_subtract_fusion.2
  300.8 11.7 %cholesky.105 = f32[128,128]{1,0:T(8,128)S(1)} custom-call(f32[128,128]{1,0:T(8,128)S(1)} %convolution_subtract_fusion.2), custom_call_target="Cholesky" | custom-call | tf_op jit(solution)/shard_map/jit(cholesky)/cholesky | solution.py:25
  312.6 0.7 compare_reduce_fusion
  314.7 0.1 triangular_solve.58
  314.7 3.9 while.1
  314.7 0.6 fusion.49
  315.3 1.3 bitcast_dynamic-update-slice_fusion.2
  316.7 0.6 fusion.49
  317.3 1.3 bitcast_dynamic-update-slice_fusion.2
  318.6 19.7 %custom-call.15 = f32[2,128,128]{1,2,0:T(8,128)S(1)} custom-call(f32[2,128,128]{2,1,0:T(8,128)S(1)} %get-tuple-element.12), custom_call_target="InvertDiagBlocksLowerTriangular" | custom-call | tf_op jit(solution)/shard_map/triangular_solve | solution.py:26
  338.3 0.6 fusion.20
  338.9 1.0 convolution_subtract_fusion.1
  339.9 0.6 fusion.23
  340.6 0.2 fusion.19
  340.7 0.0 copy-start.3
  340.7 4.5 fusion.14
  345.2 0.1 multiply_convert_fusion
  345.4 0.5 fusion.34
  345.9 5.8 %fusion.2 = bf16[4096,256]{0,1:T(8,128)(2,1)S(1)} fusion(bf16[1024,256]{0,1:T(8,128)(2,1)S(1)} %multiply_convert_fusion, bf16[4096,1024]{1,0:T(8,128)(2,1)} %param.4, bf16[4096,256]{0,1:T(8,128)(2,1)S(1)} %copy-done.3, f32[256]{0:T(256)S(1)} %bitcast.90), kind=kOutput, calls=%fused_computation.7 | convolution fusion | flops 2151677952 | bytes 13108224 | tf_op jit(solution)/shard_map/dot_general | solution.py:43
  351.7 2.7 copy.21
  354.4 20.9 %scatter_custom_fusion = bf16[8192,256]{1,0:T(8,128)(2,1)} fusion(s32[4096]{0:T(1024)S(1)} %bitcast.89, bf16[4096,256]{1,0:T(8,128)(2,1)} %copy.21, bf16[]{:T(256)} %constant.88.clone.1), kind=kCustom, calls=%fused_computation.17 | custom fusion | bytes 4194816 | tf_op jit(solution)/shard_map/scatter | solution.py:48
  375.3 96.9 %all_to_all.15 = bf16[64,1,128,256]{3,2,1,0:T(8,128)(2,1)S(1)} all-to-all(bf16[64,1,128,256]{3,2,1,0:T(8,128)(2,1)} %bitcast.80), channel_id=1, replica_groups=mesh['dp'=4,'owner'=8] {'owner'}, dimensions={0} | all-to-all | bytes 8388608 | tf_op jit(solution)/shard_map/all_to_all | solution.py:51
  472.2 2.3 copy.23
  (21 shorter events, 0.2 us)
Async XLA Ops:
  6.5 264.1 %copy-start = (f32[1024,256]{1,0:T(8,128)S(1)}, f32[1024,256]{1,0:T(8,128)}, u32[]{:S(2)}) copy-start(f32[1024,256]{1,0:T(8,128)} %param.7) | copy-start | bytes 3145732
  6.5 103.5 %all-reduce.4.cloned.1.call-start = ((), (), s32[]{:S(2)}) async-start(), calls=%async_computation.1 | async-start | bytes 8388608 | tf_op jit(solution)/shard_map/psum | solution.py:20
  21.6 88.4 %copy-start.2 = (bf16[4096,256]{1,0:T(8,128)(2,1)S(1)}, bf16[4096,256]{1,0:T(8,128)(2,1)}, u32[]{:S(2)}) copy-start(bf16[4096,256]{1,0:T(8,128)(2,1)} %param.6) | copy-start | bytes 6291460
  21.7 248.9 %all-reduce.6.cloned.1.call-start = ((), (), s32[]{:S(2)}) async-start(), calls=%async_computation.2 | async-start | bytes 8388608 | tf_op jit(solution)/shard_map/psum | solution.py:20
  110.0 2.9 copy-start.4
  338.3 2.4 copy-start.1
  340.7 5.1 %copy-start.3 = (bf16[4096,256]{0,1:T(8,128)(2,1)S(1)}, bf16[4096,256]{0,1:T(8,128)(2,1)}, u32[]{:S(2)}) copy-start(bf16[4096,256]{0,1:T(8,128)(2,1)} %copy.20) | copy-start | bytes 6291460
Sparse Core Ops, SparseCore 0:
  21.8 88.1 all-reduce.3
  113.7 156.8 all-reduce.5
